TPU v7x, 32 devices: a whole 2x2x4 slice. The times are simulated.
32 devices in a mesh: dp: 16 (over z, y, x), tensor: 2 (over core).
Axes of the slice: x: 2, y: 2, z: 4, core: 2. Of those that a mesh axis runs over, the one named last changes fastest.
Arguments:
- tokens: bfloat16 [16, 1024, 1024], P('dp', 'tensor'), may hold values from -6 to 6
- lengths: int32 [16], P('dp'), may hold values from 256 to 1024, as said below
- cotangent: bfloat16 [16, 1024, 1024], P('dp', 'tensor'), may hold values from -6 to 6
- query_key_value: float32 [1024, 3, 1024], P('dp', None, 'tensor'), may hold values from -0.1875 to 0.1875
- dense_weight: float32 [1024, 1024], P('dp', 'tensor'), may hold values from -0.75 to 0.75
- expand_weight: float32 [4096, 1024], P(('dp', 'tensor')), may hold values from -0.1875 to 0.1875
- shrink_weight: float32 [4096, 1024], P(('dp', 'tensor')), may hold values from -0.09375 to 0.09375
- query_value_bias: float32 [2, 1024], P(None, 'tensor'), may hold values from -1.8 to 1.8
- expand_bias: float32 [4096], P(('dp', 'tensor')), may hold values from -1.8 to 1.8
- small_params: float32 [6, 1024], P(None, ('dp', 'tensor')), may hold values from -1.5 to 1.5, as said below
- query_key_value_moment: float32 [1024, 3, 1024], P('dp', None, 'tensor'), may hold values from -23.04 to 23.04
- dense_moment: float32 [1024, 1024], P('dp', 'tensor'), may hold values from -23.04 to 23.04
- expand_moment: float32 [4096, 1024], P(('dp', 'tensor')), may hold values from -23.04 to 23.04
- shrink_moment: float32 [4096, 1024], P(('dp', 'tensor')), may hold values from -23.04 to 23.04
- small_first: float32 [6, 1024], P(None, ('dp', 'tensor')), may hold values from -7.68 to 7.68
- small_second: float32 [6, 1024], P(None, ('dp', 'tensor')), may hold values from 1.6384 to 16.384
- bias_first: float32 [2, 1024], P(None, 'tensor'), may hold values from -7.68 to 7.68
- bias_second: float32 [2, 1024], P(None, 'tensor'), may hold values from 1.6384 to 16.384
- expand_first: float32 [4096], P(('dp', 'tensor')), may hold values from -7.68 to 7.68
- expand_second: float32 [4096], P(('dp', 'tensor')), may hold values from 1.6384 to 16.384
- step_count: int32 [1], replicated, may hold values from 1 to 3
Outputs:
- output: bfloat16 [16, 1024, 1024], P('dp', 'tensor')
- input_grad: float32 [16, 1024, 1024], P('dp', 'tensor')
- query_key_value_grad: float32 [1024, 3, 1024], P('dp', None, 'tensor')
- dense_grad: float32 [1024, 1024], P('dp', 'tensor')
- expand_grad: float32 [4096, 1024], P(('dp', 'tensor'))
- shrink_grad: float32 [4096, 1024], P(('dp', 'tensor'))
- query_value_bias_grad: float32 [2, 1024], P(None, 'tensor')
- expand_bias_grad: float32 [4096], P(('dp', 'tensor'))
- small_params_grad: float32 [6, 1024], P(None, ('dp', 'tensor'))
- query_key_value_new: float32 [1024, 3, 1024], P('dp', None, 'tensor')
- dense_new: float32 [1024, 1024], P('dp', 'tensor')
- expand_new: float32 [4096, 1024], P(('dp', 'tensor'))
- shrink_new: float32 [4096, 1024], P(('dp', 'tensor'))
- query_value_bias_new: float32 [2, 1024], P(None, 'tensor')
- expand_bias_new: float32 [4096], P(('dp', 'tensor'))
- small_params_new: float32 [6, 1024], P(None, ('dp', 'tensor'))
- query_key_value_moment_new: float32 [1024, 3, 1024], P('dp', None, 'tensor')
- dense_moment_new: float32 [1024, 1024], P('dp', 'tensor')
- expand_moment_new: float32 [4096, 1024], P(('dp', 'tensor'))
- shrink_moment_new: float32 [4096, 1024], P(('dp', 'tensor'))
- small_first_new: float32 [6, 1024], P(None, ('dp', 'tensor'))
- small_second_new: float32 [6, 1024], P(None, ('dp', 'tensor'))
- bias_first_new: float32 [2, 1024], P(None, 'tensor')
- bias_second_new: float32 [2, 1024], P(None, 'tensor')
- expand_first_new: float32 [4096], P(('dp', 'tensor'))
- expand_second_new: float32 [4096], P(('dp', 'tensor'))
Inputs may be any that keep to these rules, and one draw needn't show every extreme that they name: `lengths`: in every draw one sequence has 1024 valid positions and another a quarter of 1024. `small_params`: rows 0 and 3 lie within 0.5 to 1.5.
All inputs are finite; a program needn't handle non-finite values.
Results may differ from a plain program's by a relative error of at most 0.012.
The roundings to bfloat16 on the way count: a program that leaves them out, or rounds other values in their place, can miss the bound.
Values may be sent and summed in bfloat16 or wider, within the bound.
No kernel may reach another device: no remote copies, remote signals or barrier semaphores. Data moves between devices by JAX's collectives and lax.ppermute only.
A program may use at most 192 MiB of HBM per device.

v0:
```python
import math

import jax
import jax.numpy as jnp
from jax import lax
from jax.sharding import PartitionSpec as P

H = 16
HD = 64
FF = 4096


layer_eps = 1e-05
muon_eps = 1e-07
adam_eps = 1e-08
decay_rate = 0.95
muon_rate = 0.25
adam_rate = 0.2
beta_first = 0.9
beta_second = 0.999
first_coef = 3.4445
second_coef = -4.775
third_coef = 2.0315
highest = lax.Precision.HIGHEST
contract_last = (((1,), (1,)), ((), ()))
contract_first = (((0,), (0,)), ((), ()))


def normalize(values):
    centered = values - jnp.mean(values, axis=-1, keepdims=True)
    inverse = lax.rsqrt(jnp.mean(centered * centered, axis=-1, keepdims=True) + layer_eps)
    return (centered * inverse, inverse)


def norm_back(upstream, normed, inverse, gain):
    scaled = upstream * gain
    return inverse * (
        scaled
        - jnp.mean(scaled, axis=-1, keepdims=True)
        - normed * jnp.mean(scaled * normed, axis=-1, keepdims=True)
    )


def gelu_slope(values):
    inner = jnp.tanh(0.7978845608028654 * (values + 0.044715 * values**3))
    return 0.5 * (1.0 + inner) + 0.5 * values * (1.0 - inner * inner) * 0.7978845608028654 * (
        1.0 + 3.0 * 0.044715 * values * values
    )


def score_block(query_block, keys, rows, length, slopes):
    scores = jnp.einsum(
        "qhc,khc->hqk", query_block, keys, preferred_element_type=jnp.float32
    ) * keys.shape[-1] ** (-0.5)
    columns = jnp.arange(keys.shape[0], dtype=jnp.int32)
    offset = (rows[:, None] - columns[None, :]).astype(jnp.float32)
    allowed = (columns[None, :] <= rows[:, None]) & (columns[None, :] < length)
    return jnp.where(allowed[None], scores - slopes[:, None, None] * offset[None], -1e30)


def attend(queries, keys, values, length, slopes, block):
    count = queries.shape[0] // block

    def one(index):
        begin = index * block
        query_block = lax.dynamic_slice_in_dim(queries, begin, block, 0)
        rows = begin + jnp.arange(block, dtype=jnp.int32)
        scores = score_block(query_block, keys, rows, length, slopes)
        peak = jnp.max(scores, axis=-1, keepdims=True)
        weights = jnp.exp(scores - peak)
        total = jnp.sum(weights, axis=-1, keepdims=True)
        mixed = jnp.einsum(
            "hqk,khc->qhc",
            (weights / total).astype(jnp.bfloat16),
            values,
            preferred_element_type=jnp.float32,
        )
        return (mixed.astype(jnp.bfloat16), (peak + jnp.log(total))[:, :, 0])

    mixed, logsum = lax.map(one, jnp.arange(count, dtype=jnp.int32))
    return (mixed.reshape(queries.shape), logsum)


def attend_back(queries, keys, values, grad_mixed, logsum, length, slopes, block):
    count = queries.shape[0] // block
    scale = queries.shape[-1] ** (-0.5)

    def one(carry, index):
        key_total, value_total = carry
        begin = index * block
        query_block = lax.dynamic_slice_in_dim(queries, begin, block, 0)
        grad_block = lax.dynamic_slice_in_dim(grad_mixed, begin, block, 0)
        rows = begin + jnp.arange(block, dtype=jnp.int32)
        scores = score_block(query_block, keys, rows, length, slopes)
        probs = jnp.exp(scores - logsum[index][:, :, None])
        grad_probs = jnp.einsum(
            "qhc,khc->hqk", grad_block, values, preferred_element_type=jnp.float32
        )
        inner = jnp.sum(probs * grad_probs, axis=-1, keepdims=True)
        grad_scores = (probs * (grad_probs - inner)).astype(jnp.bfloat16)
        grad_query = (
            jnp.einsum("hqk,khc->qhc", grad_scores, keys, preferred_element_type=jnp.float32)
            * scale
        )
        key_total = (
            key_total
            + jnp.einsum(
                "hqk,qhc->khc", grad_scores, query_block, preferred_element_type=jnp.float32
            )
            * scale
        )
        value_total = value_total + jnp.einsum(
            "hqk,qhc->khc",
            probs.astype(jnp.bfloat16),
            grad_block,
            preferred_element_type=jnp.float32,
        )
        return ((key_total, value_total), grad_query.astype(jnp.bfloat16))

    empty = jnp.zeros(keys.shape, jnp.float32)
    (key_total, value_total), grad_query = lax.scan(
        one, (empty, empty), jnp.arange(count, dtype=jnp.int32)
    )
    return (
        grad_query.reshape(queries.shape),
        key_total.astype(jnp.bfloat16),
        value_total.astype(jnp.bfloat16),
    )


def block_gram(ortho):
    return jnp.einsum("rbi,rbj->bij", ortho, ortho, precision=highest)


def block_step(ortho, gram):
    product = jnp.einsum("rbi,bij->rbj", ortho, gram, precision=highest)
    twice = jnp.einsum("rbi,bij->rbj", product, gram, precision=highest)
    return first_coef * ortho + second_coef * product + third_coef * twice


def feed_gram(ortho):
    return lax.psum(block_gram(ortho), ("dp", "tensor"))


def adam_step(param, gradient, first, second, count):
    first_new = beta_first * first + (1.0 - beta_first) * gradient
    second_new = beta_second * second + (1.0 - beta_second) * gradient * gradient
    corr_one = 1.0 - jnp.power(beta_first, count)
    corr_two = 1.0 - jnp.power(beta_second, count)
    change = adam_rate * (first_new / corr_one) / (jnp.sqrt(second_new / corr_two) + adam_eps)
    return (param - change, first_new, second_new)


def per_device(
    tokens,
    lengths,
    cotangent,
    query_key_value,
    dense_weight,
    expand_weight,
    shrink_weight,
    query_value_bias,
    expand_bias,
    small_params,
    query_key_value_moment,
    dense_moment,
    expand_moment,
    shrink_moment,
    small_first,
    small_second,
    bias_first,
    bias_second,
    expand_first,
    expand_second,
    step_count,
):
    pieces = lax.axis_size("tensor")
    local_rows = tokens.shape[1]
    seq_rows = local_rows * pieces
    width = tokens.shape[2]
    head_cols = query_key_value.shape[2]
    heads_here = head_cols // HD
    block = min(512, seq_rows)
    length = lengths[0]
    here = lax.axis_index("tensor")
    positions = here * local_rows + jnp.arange(local_rows, dtype=jnp.int32)
    valid = (positions < length).astype(jnp.float32)[:, None]
    head_index = here * heads_here + jnp.arange(heads_here, dtype=jnp.int32) + 1
    slopes = jnp.exp2(-8.0 * head_index.astype(jnp.float32) / H)
    low_triple = query_key_value.astype(jnp.bfloat16)
    low_dense = dense_weight.astype(jnp.bfloat16)
    low_expand = expand_weight.astype(jnp.bfloat16)
    low_shrink = shrink_weight.astype(jnp.bfloat16)
    low_shift = expand_bias.astype(jnp.bfloat16)
    triple, dense, expand, shrink, expand_shift = (
        lax.all_gather(low_triple, "dp", axis=0, tiled=True),
        lax.all_gather(low_dense, "dp", axis=0, tiled=True),
        lax.all_gather(low_expand, "dp", axis=0, tiled=True),
        lax.all_gather(low_shrink, "dp", axis=0, tiled=True),
        lax.all_gather(low_shift, "dp", axis=0, tiled=True),
    )
    small = lax.all_gather(
        small_params.astype(jnp.bfloat16), ("dp", "tensor"), axis=1, tiled=True
    ).astype(jnp.float32)
    query_shift = lax.optimization_barrier(query_value_bias.astype(jnp.bfloat16)).astype(
        jnp.float32
    )
    shift_values = expand_shift.astype(jnp.float32)
    inputs = tokens[0].astype(jnp.float32)
    normed_one, inverse_one = normalize(inputs)
    hidden_one = lax.all_gather(
        (normed_one * small[0] + small[1]).astype(jnp.bfloat16), "tensor", axis=0, tiled=True
    )
    projected = jnp.einsum("sd,dkc->skc", hidden_one, triple, preferred_element_type=jnp.float32)
    queries = (
        (projected[:, 0] + query_shift[0]).astype(jnp.bfloat16).reshape(seq_rows, heads_here, HD)
    )
    keys = projected[:, 1].astype(jnp.bfloat16).reshape(seq_rows, heads_here, HD)
    values = (
        (projected[:, 2] + query_shift[1]).astype(jnp.bfloat16).reshape(seq_rows, heads_here, HD)
    )
    mixed, logsum = attend(queries, keys, values, length, slopes, block)
    mixed_flat = mixed.reshape(seq_rows, head_cols)
    residual = inputs + (
        lax.psum_scatter(
            lax.dot_general(mixed_flat, dense, contract_last, preferred_element_type=jnp.float32),
            "tensor",
            scatter_dimension=0,
            tiled=True,
        )
        + small[2]
    )
    normed_two, inverse_two = normalize(residual)
    hidden_local = (normed_two * small[3] + small[4]).astype(jnp.bfloat16)
    grad_result = valid * cotangent[0].astype(jnp.float32)
    grad_feed = grad_result.astype(jnp.bfloat16)
    hidden_two = lax.all_gather(hidden_local, "tensor", axis=0, tiled=True)
    expanded = (
        lax.dot_general(hidden_two, expand, contract_last, preferred_element_type=jnp.float32)
        + shift_values
    )
    activated = jax.nn.gelu(expanded, approximate=True).astype(jnp.bfloat16)
    feed = lax.psum_scatter(
        jnp.dot(activated, shrink, preferred_element_type=jnp.float32),
        "tensor",
        scatter_dimension=0,
        tiled=True,
    )
    grad_feed_all = lax.all_gather(grad_feed, "tensor", axis=0, tiled=True)
    grad_act = lax.dot_general(
        grad_feed_all, shrink, contract_last, preferred_element_type=jnp.float32
    )
    shrink_grad = lax.dot_general(
        activated, grad_feed_all, contract_first, preferred_element_type=jnp.float32
    )
    grad_expanded = (grad_act * gelu_slope(expanded)).astype(jnp.bfloat16)
    expand_grad = lax.dot_general(
        grad_expanded, hidden_two, contract_first, preferred_element_type=jnp.float32
    )
    grad_hidden_two = lax.psum_scatter(
        jnp.dot(grad_expanded, expand, preferred_element_type=jnp.float32),
        "tensor",
        scatter_dimension=0,
        tiled=True,
    )
    shift_grad = jnp.sum(grad_expanded.astype(jnp.float32), axis=0)
    output = (valid * (residual + (feed + small[5]))).astype(jnp.bfloat16)[None]
    grad_residual = grad_result + norm_back(grad_hidden_two, normed_two, inverse_two, small[3])
    grad_branch = grad_residual.astype(jnp.bfloat16)
    grad_branch_all = lax.all_gather(grad_branch, "tensor", axis=0, tiled=True)
    dense_grad = lax.dot_general(
        grad_branch_all, mixed_flat, contract_first, preferred_element_type=jnp.float32
    )
    grad_mixed = (
        jnp.dot(grad_branch_all, dense, preferred_element_type=jnp.float32)
        .astype(jnp.bfloat16)
        .reshape(seq_rows, heads_here, HD)
    )
    grad_queries, grad_keys, grad_values = attend_back(
        queries, keys, values, grad_mixed, logsum, length, slopes, block
    )
    grad_projected = jnp.stack((grad_queries, grad_keys, grad_values), axis=1).reshape(
        seq_rows, 3, head_cols
    )
    bias_grad_local = jnp.sum(grad_projected[:, 0::2].astype(jnp.float32), axis=0)
    triple_grad = jnp.einsum(
        "sd,skc->dkc", hidden_one, grad_projected, preferred_element_type=jnp.float32
    )
    grad_hidden_one = lax.psum_scatter(
        jnp.einsum("skc,dkc->sd", grad_projected, triple, preferred_element_type=jnp.float32),
        "tensor",
        scatter_dimension=0,
        tiled=True,
    )
    input_grad = grad_residual + norm_back(grad_hidden_one, normed_one, inverse_one, small[0])
    small_terms = jnp.stack(
        (
            jnp.sum(grad_hidden_one * normed_one, axis=0),
            jnp.sum(grad_hidden_one, axis=0),
            jnp.sum(grad_branch.astype(jnp.float32), axis=0),
            jnp.sum(grad_hidden_two * normed_two, axis=0),
            jnp.sum(grad_hidden_two, axis=0),
            jnp.sum(grad_feed.astype(jnp.float32), axis=0),
        )
    )
    small_grad = lax.psum_scatter(small_terms, ("dp", "tensor"), scatter_dimension=1, tiled=True)
    triple_sum, dense_sum, expand_sum, shrink_sum, shift_sum = (
        lax.psum_scatter(triple_grad, "dp", scatter_dimension=0, tiled=True),
        lax.psum_scatter(dense_grad, "dp", scatter_dimension=0, tiled=True),
        lax.psum_scatter(expand_grad, "dp", scatter_dimension=0, tiled=True),
        lax.psum_scatter(shrink_grad, "dp", scatter_dimension=0, tiled=True),
        lax.psum_scatter(shift_grad, "dp", scatter_dimension=0, tiled=True),
    )
    count = step_count[0].astype(jnp.float32)
    rows_here = triple_sum.shape[0]
    triple_moment = decay_rate * query_key_value_moment + triple_sum
    dense_moment_new = decay_rate * dense_moment + dense_sum
    expand_moment_new = decay_rate * expand_moment + expand_sum
    shrink_moment_new = decay_rate * shrink_moment + shrink_sum
    head_update = jnp.concatenate(
        (
            (triple_sum + decay_rate * triple_moment).reshape(rows_here, 3 * heads_here, HD),
            (dense_sum + decay_rate * dense_moment_new).reshape(rows_here, heads_here, HD),
        ),
        axis=1,
    )
    feed_rows = expand_sum.shape[0]
    feed_blocks = width // HD
    feed_update = jnp.stack(
        (expand_sum + decay_rate * expand_moment_new, shrink_sum + decay_rate * shrink_moment_new)
    )
    feed_update = (
        feed_update.reshape(2, feed_rows, feed_blocks, HD)
        .transpose(1, 0, 2, 3)
        .reshape(feed_rows, 2 * feed_blocks, HD)
    )
    raw_head, bias_sum = lax.psum((block_gram(head_update), bias_grad_local), "dp")
    head_scale = jnp.sqrt(jnp.trace(raw_head, axis1=1, axis2=2)) + muon_eps
    head_ortho = head_update / head_scale[None, :, None]
    head_grams = [raw_head / (head_scale * head_scale)[:, None, None]]
    raw_feed = feed_gram(feed_update)
    feed_scale = jnp.sqrt(jnp.trace(raw_feed, axis1=1, axis2=2)) + muon_eps
    feed_ortho = feed_update / feed_scale[None, :, None]
    feed_grams = [raw_feed / (feed_scale * feed_scale)[:, None, None]]
    for turn in range(5):
        if turn >= len(head_grams):
            head_grams.append(lax.psum(block_gram(head_ortho), "dp"))
            feed_grams.append(feed_gram(feed_ortho))
        head_ortho = block_step(head_ortho, head_grams[turn])
        feed_ortho = block_step(feed_ortho, feed_grams[turn])
    head_change = head_ortho * (muon_rate * math.sqrt(max(1.0, width / HD)))
    triple_new = query_key_value - head_change[:, : 3 * heads_here].reshape(rows_here, 3, head_cols)
    dense_new = dense_weight - head_change[:, 3 * heads_here :].reshape(rows_here, head_cols)
    feed_change = feed_ortho * (muon_rate * math.sqrt(max(1.0, FF / HD)))
    feed_change = (
        feed_change.reshape(feed_rows, 2, feed_blocks, HD)
        .transpose(1, 0, 2, 3)
        .reshape(2, feed_rows, width)
    )
    expand_new = expand_weight - feed_change[0]
    shrink_new = shrink_weight - feed_change[1]
    small_new, small_first_new, small_second_new = adam_step(
        small_params, small_grad, small_first, small_second, count
    )
    bias_new, bias_first_new, bias_second_new = adam_step(
        query_value_bias, bias_sum, bias_first, bias_second, count
    )
    shift_new, expand_first_new, expand_second_new = adam_step(
        expand_bias, shift_sum, expand_first, expand_second, count
    )
    return (
        output,
        input_grad[None],
        triple_sum,
        dense_sum,
        expand_sum,
        shrink_sum,
        bias_sum,
        shift_sum,
        small_grad,
        triple_new,
        dense_new,
        expand_new,
        shrink_new,
        bias_new,
        shift_new,
        small_new,
        triple_moment,
        dense_moment_new,
        expand_moment_new,
        shrink_moment_new,
        small_first_new,
        small_second_new,
        bias_first_new,
        bias_second_new,
        expand_first_new,
        expand_second_new,
    )


def solution(mesh):
    in_specs = (
        P("dp", "tensor", None),
        P("dp"),
        P("dp", "tensor", None),
        P("dp", None, "tensor"),
        P("dp", "tensor"),
        P(("dp", "tensor"), None),
        P(("dp", "tensor"), None),
        P(None, "tensor"),
        P(("dp", "tensor")),
        P(None, ("dp", "tensor")),
        P("dp", None, "tensor"),
        P("dp", "tensor"),
        P(("dp", "tensor"), None),
        P(("dp", "tensor"), None),
        P(None, ("dp", "tensor")),
        P(None, ("dp", "tensor")),
        P(None, "tensor"),
        P(None, "tensor"),
        P(("dp", "tensor")),
        P(("dp", "tensor")),
        P(),
    )
    out_specs = (
        P("dp", "tensor", None),
        P("dp", "tensor", None),
        P("dp", None, "tensor"),
        P("dp", "tensor"),
        P(("dp", "tensor"), None),
        P(("dp", "tensor"), None),
        P(None, "tensor"),
        P(("dp", "tensor")),
        P(None, ("dp", "tensor")),
        P("dp", None, "tensor"),
        P("dp", "tensor"),
        P(("dp", "tensor"), None),
        P(("dp", "tensor"), None),
        P(None, "tensor"),
        P(("dp", "tensor")),
        P(None, ("dp", "tensor")),
        P("dp", None, "tensor"),
        P("dp", "tensor"),
        P(("dp", "tensor"), None),
        P(("dp", "tensor"), None),
        P(None, ("dp", "tensor")),
        P(None, ("dp", "tensor")),
        P(None, "tensor"),
        P(None, "tensor"),
        P(("dp", "tensor")),
        P(("dp", "tensor")),
    )
    return jax.shard_map(
        per_device, mesh=mesh, in_specs=in_specs, out_specs=out_specs, check_vma=False
    )
```

profile of v0, /device:TPU:0, one launch (start us, length us, event | category | flops | bytes accessed | tf_op | source)
XLA Modules:
  0.0 2482.1 jit_solution(18238868421991019305)
XLA Ops:
  8.0 43.4 %all-gather = bf16[32,32,6]{1,2,0:T(8,128)(2,1)S(1)} all-gather(bf16[1,32,6]{1,2,0:T(8,128)(2,1)S(1)} %convert_bitcast_fusion.1), channel_id=1, replica_groups=mesh['dp'=16,'tensor'=2] {'dp','tensor'}, dimensions={0}, use_global_device_ids=true | all-gather | bytes 12672 | tf_op jit(solution)/shard_map/all_gather | solution.py:202
  62.9 72.4 %all-gather.13.cloned.1.call-done = bf16[1024,3,512]{2,0,1:T(8,128)(2,1)} async-done(((bf16[64,3,512]{2,0,1:T(8,128)(2,1)}), bf16[1024,3,512]{2,0,1:T(8,128)(2,1)}) %all-gather.13.cloned.1.call-update) | async-done | bytes 3145744 | tf_op jit(solution)/shard_map/all_gather | solution.py:196
  143.4 30.9 %while.28 = (s32[]{:T(128)}, bf16[2,512,8,64]{1,3,2,0:T(8,128)(2,1)}, f32[2,8,512]{2,1,0:T(8,128)S(1)}, s32[2]{0:T(128)S(1)}, s32[]{:T(128)}, /*index=5*/bf16[10...) while((s32[]{:T(128)}, ...), condition=%wide.region_5.6_spmd.clone, body=%wide.region_2.5_spmd.clone.sunk | while | flops 1118041600 | bytes 58860780 | solution.py:80
  216.9 41.5 %all-gather.1 = bf16[16,1,128]{2,1,0:T(2,128)(2,1)S(1)} all-gather(bf16[1,1,128]{2,1,0:T(2,128)(2,1)S(1)} %convert_bitcast_fusion.2), channel_id=1, replica_groups=mesh['dp'=16,'tensor'=2] {'dp'}, dimensions={0}, use_global_device_ids=true | all-gather | bytes 4352 | tf_op jit(solution)/shard_map/all_gather | solution.py:200
  258.4 30.1 %all-gather.19.cloned.1.call-done = bf16[2048,1024]{1,0:T(8,128)(2,1)} async-done(((bf16[128,1024]{1,0:T(8,128)(2,1)}), bf16[2048,1024]{1,0:T(8,128)(2,1)}) %all-gather.19.cloned.1.call-update) | async-done | bytes 4194320 | tf_op jit(solution)/shard_map/all_gather | solution.py:198
  313.5 80.1 %all-gather.21.cloned.1.call-done = bf16[2048,1024]{1,0:T(8,128)(2,1)} async-done(((bf16[128,1024]{1,0:T(8,128)(2,1)}), bf16[2048,1024]{1,0:T(8,128)(2,1)}) %all-gather.21.cloned.1.call-update) | async-done | bytes 4194320 | tf_op jit(solution)/shard_map/all_gather | solution.py:199
  489.4 122.2 %while.29 = (s32[]{:T(128)}, f32[1024,8,64]{0,2,1:T(8,128)S(1)}, f32[1024,8,64]{0,2,1:T(8,128)}, bf16[2,512,8,64]{1,3,2,0:T(8,128)(2,1)}, s32[2]{0:T(128)S(1)}, ...) while((s32[]{:T(128)}, f32[1024,8,64]{0,2,1:T(8,128)S(1)}, ...), condition=%wide.region_15.16_spmd.clone, body=%wide.region_13.15_spmd.clone.sunk | while | flops 2735732224 | bytes 212427632 | solution.py:121
  517.9 15.0 multiply_convert_fusion.4
  578.3 15.1 multiply_convert_fusion.4
  648.3 77.8 %all-reduce.1 = (f32[2,512]{1,0:T(2,128)S(1)}, f32[2048]{0:T(1024)S(1)}) all-reduce(f32[2,512]{1,0:T(2,128)S(1)} %convert_reduce_fusion.1, f32[2048]{0:T(1024)S(1)} %copy-done.53), channel_id=1, replica_groups=mesh['dp'=16,'tensor'=2] {'dp'}, use_global_device_ids=true, to_apply=%region_24.25 | all-reduce | flops 3072 | bytes 24576 | tf_op jit(solution)/shard_map/psum | solution.py:337
  731.2 177.4 %reduce-scatter.26.cloned.1.call-done = f32[128,1024]{1,0:T(8,128)} async-done(((f32[2048,1024]{1,0:T(8,128)}), f32[128,1024]{1,0:T(8,128)}) %reduce-scatter.26.cloned.1.call-update) | async-done | bytes 524304 | tf_op jit(solution)/shard_map/reduce_scatter | solution.py:311
  911.0 14.3 reduce-scatter.18.cloned.1.call-done
  932.2 133.4 %reduce-scatter.20.cloned.1.call-done = f32[64,3,512]{2,0,1:T(8,128)} async-done(((f32[1024,3,512]{2,0,1:T(8,128)}), f32[64,3,512]{2,0,1:T(8,128)}) %reduce-scatter.20.cloned.1.call-update) | async-done | bytes 393232 | tf_op jit(solution)/shard_map/reduce_scatter | solution.py:308
  1077.4 128.0 %reduce-scatter.28.cloned.1.call-done = f32[32,6]{1,0:T(8,128)} async-done(((f32[1024,6]{1,0:T(8,128)}), f32[32,6]{1,0:T(8,128)}) %reduce-scatter.28.cloned.1.call-update) | async-done | bytes 784
  1206.9 130.1 %all-reduce.23.cloned.1.call-done = f32[32,64,64]{2,1,0:T(8,128)} async-done(((f32[32,64,64]{2,1,0:T(8,128)}), f32[32,64,64]{2,1,0:T(8,128)}) %all-reduce.23.cloned.1.call-update) | async-done | bytes 524304 | tf_op jit(solution)/shard_map/psum | solution.py:142
  1337.0 116.6 %all-reduce.13.cloned.1.call-done = f32[32,64,64]{2,1,0:T(8,128)} async-done(((f32[32,64,64]{2,1,0:T(8,128)}), f32[32,64,64]{2,1,0:T(8,128)}) %all-reduce.13.cloned.1.call-update) | async-done | bytes 524304 | tf_op jit(solution)/shard_map/psum | solution.py:337
  1466.8 125.6 %all-reduce.25.cloned.1.call-done = f32[32,64,64]{2,1,0:T(8,128)} async-done(((f32[32,64,64]{2,1,0:T(8,128)}), f32[32,64,64]{2,1,0:T(8,128)}) %all-reduce.25.cloned.1.call-update) | async-done | bytes 524304 | tf_op jit(solution)/shard_map/psum | solution.py:142
  1603.4 126.7 %all-reduce.27.cloned.1.call-done = f32[32,64,64]{2,1,0:T(8,128)} async-done(((f32[32,64,64]{2,1,0:T(8,128)}), f32[32,64,64]{2,1,0:T(8,128)}) %all-reduce.27.cloned.1.call-update) | async-done | bytes 524304 | tf_op jit(solution)/shard_map/psum | solution.py:142
  1738.0 108.7 %all-reduce.15.cloned.1.call-done = f32[32,64,64]{2,1,0:T(8,128)} async-done(((f32[32,64,64]{2,1,0:T(8,128)}), f32[32,64,64]{2,1,0:T(8,128)}) %all-reduce.15.cloned.1.call-update) | async-done | bytes 524304 | tf_op jit(solution)/shard_map/psum | solution.py:347
  1853.5 128.2 %all-reduce.29.cloned.1.call-done = f32[32,64,64]{2,1,0:T(8,128)} async-done(((f32[32,64,64]{2,1,0:T(8,128)}), f32[32,64,64]{2,1,0:T(8,128)}) %all-reduce.29.cloned.1.call-update) | async-done | bytes 524304 | tf_op jit(solution)/shard_map/psum | solution.py:142
  1989.7 108.5 %all-reduce.17.cloned.1.call-done = f32[32,64,64]{2,1,0:T(8,128)} async-done(((f32[32,64,64]{2,1,0:T(8,128)}), f32[32,64,64]{2,1,0:T(8,128)}) %all-reduce.17.cloned.1.call-update) | async-done | bytes 524304 | tf_op jit(solution)/shard_map/psum | solution.py:347
  2105.0 128.1 %all-reduce.31.cloned.1.call-done = f32[32,64,64]{2,1,0:T(8,128)} async-done(((f32[32,64,64]{2,1,0:T(8,128)}), f32[32,64,64]{2,1,0:T(8,128)}) %all-reduce.31.cloned.1.call-update) | async-done | bytes 524304 | tf_op jit(solution)/shard_map/psum | solution.py:142
  2239.2 110.5 %all-reduce.19.cloned.1.call-done = f32[32,64,64]{2,1,0:T(8,128)} async-done(((f32[32,64,64]{2,1,0:T(8,128)}), f32[32,64,64]{2,1,0:T(8,128)}) %all-reduce.19.cloned.1.call-update) | async-done | bytes 524304 | tf_op jit(solution)/shard_map/psum | solution.py:347
  2359.4 108.4 %all-reduce.21.cloned.1.call-done = f32[32,64,64]{2,1,0:T(8,128)} async-done(((f32[32,64,64]{2,1,0:T(8,128)}), f32[32,64,64]{2,1,0:T(8,128)}) %all-reduce.21.cloned.1.call-update) | async-done | bytes 524304 | tf_op jit(solution)/shard_map/psum | solution.py:347
  (382 shorter events, 436.8 us)
Async XLA Ops:
  56.1 79.2 %all-gather.13.cloned.1.call-start = ((), (), s32[]{:S(2)}) async-start(), calls=%async_computation.10 | async-start | bytes 3342336 | tf_op jit(solution)/shard_map/all_gather | solution.py:196
  56.9 135.5 %all-gather.15.cloned.1.call-start = ((), (), s32[]{:S(2)}) async-start(), calls=%async_computation.11 | async-start | bytes 1114112 | tf_op jit(solution)/shard_map/all_gather | solution.py:197
  57.6 150.7 %reduce-scatter.12.cloned.1.call-start = ((), (), s32[]{:S(2)}) async-start(), calls=%async_computation.12 | async-start | bytes 6291456 | tf_op jit(solution)/shard_map/reduce_scatter | solution.py:225
  197.3 91.2 %all-gather.19.cloned.1.call-start = ((), (), s32[]{:S(2)}) async-start(), calls=%async_computation.14 | async-start | bytes 4456448 | tf_op jit(solution)/shard_map/all_gather | solution.py:198
  199.0 100.6 %all-gather.17.cloned.1.call-start = ((), (), s32[]{:S(2)}) async-start(), calls=%async_computation.13 | async-start | bytes 3145728 | tf_op jit(solution)/shard_map/all_gather | solution.py:237
  212.3 101.2 %all-gather.23.cloned.1.call-start = ((), (), s32[]{:S(2)}) async-start(), calls=%async_computation.17 | async-start | bytes 3145728 | tf_op jit(solution)/shard_map/all_gather | solution.py:249
  215.0 178.7 %all-gather.21.cloned.1.call-start = ((), (), s32[]{:S(2)}) async-start(), calls=%async_computation.15 | async-start | bytes 4456448 | tf_op jit(solution)/shard_map/all_gather | solution.py:199
  216.8 209.1 %reduce-scatter.16.cloned.1.call-start = ((), (), s32[]{:S(2)}) async-start(), calls=%async_computation.18 | async-start | bytes 6291456 | tf_op jit(solution)/shard_map/reduce_scatter | solution.py:260
  446.3 281.0 %reduce-scatter.22.cloned.1.call-start = ((), (), s32[]{:S(2)}) async-start(), calls=%async_computation.22 | async-start | bytes 2228224 | tf_op jit(solution)/shard_map/reduce_scatter | solution.py:309
  462.8 266.2 %reduce-scatter.24.cloned.1.call-start = ((), (), s32[]{:S(2)}) async-start(), calls=%async_computation.23 | async-start | bytes 8912896 | tf_op jit(solution)/shard_map/reduce_scatter | solution.py:310
  473.5 435.2 %reduce-scatter.26.cloned.1.call-start = ((), (), s32[]{:S(2)}) async-start(), calls=%async_computation.24 | async-start | bytes 8912896 | tf_op jit(solution)/shard_map/reduce_scatter | solution.py:311
  484.1 441.2 %reduce-scatter.18.cloned.1.call-start = ((), (), s32[]{:S(2)}) async-start(), calls=%async_computation.20 | async-start | bytes 6291456 | tf_op jit(solution)/shard_map/reduce_scatter | solution.py:289
  632.8 432.8 %reduce-scatter.20.cloned.1.call-start = ((), (), s32[]{:S(2)}) async-start(), calls=%async_computation.21 | async-start | bytes 6684672 | tf_op jit(solution)/shard_map/reduce_scatter | solution.py:308
  641.1 564.3 %reduce-scatter.28.cloned.1.call-start = ((), (), s32[]{:S(2)}) async-start(), calls=%async_computation.35 | async-start | bytes 540672
  929.0 408.0 %all-reduce.23.cloned.1.call-start = ((), (), s32[]{:S(2)}) async-start(), calls=%async_computation.30 | async-start | bytes 2097152 | tf_op jit(solution)/shard_map/psum | solution.py:142
  931.9 521.7 %all-reduce.13.cloned.1.call-start = ((), (), s32[]{:S(2)}) async-start(), calls=%async_computation.25 | async-start | bytes 2097152 | tf_op jit(solution)/shard_map/psum | solution.py:337
  1073.1 519.3 %all-reduce.25.cloned.1.call-start = ((), (), s32[]{:S(2)}) async-start(), calls=%async_computation.31 | async-start | bytes 2097152 | tf_op jit(solution)/shard_map/psum | solution.py:142
  1462.5 267.6 %all-reduce.27.cloned.1.call-start = ((), (), s32[]{:S(2)}) async-start(), calls=%async_computation.32 | async-start | bytes 2097152 | tf_op jit(solution)/shard_map/psum | solution.py:142
  1600.3 246.4 %all-reduce.15.cloned.1.call-start = ((), (), s32[]{:S(2)}) async-start(), calls=%async_computation.26 | async-start | bytes 2097152 | tf_op jit(solution)/shard_map/psum | solution.py:347
  1603.2 378.5 %all-reduce.29.cloned.1.call-start = ((), (), s32[]{:S(2)}) async-start(), calls=%async_computation.33 | async-start | bytes 2097152 | tf_op jit(solution)/shard_map/psum | solution.py:142
  1738.0 360.2 %all-reduce.17.cloned.1.call-start = ((), (), s32[]{:S(2)}) async-start(), calls=%async_computation.27 | async-start | bytes 2097152 | tf_op jit(solution)/shard_map/psum | solution.py:347
  1853.3 379.9 %all-reduce.31.cloned.1.call-start = ((), (), s32[]{:S(2)}) async-start(), calls=%async_computation.34 | async-start | bytes 2097152 | tf_op jit(solution)/shard_map/psum | solution.py:142
  1989.6 360.0 %all-reduce.19.cloned.1.call-start = ((), (), s32[]{:S(2)}) async-start(), calls=%async_computation.28 | async-start | bytes 2097152 | tf_op jit(solution)/shard_map/psum | solution.py:347
  2104.7 363.1 %all-reduce.21.cloned.1.call-start = ((), (), s32[]{:S(2)}) async-start(), calls=%async_computation.29 | async-start | bytes 2097152 | tf_op jit(solution)/shard_map/psum | solution.py:347
  (72 other events, 2850.0 us)
Sparse Core Ops, SparseCore 0:
  66.3 69.0 all-gather.12
  138.7 53.6 all-gather.14
  197.4 10.8 reduce-scatter.11
  211.5 76.9 all-gather.18
  301.7 11.7 all-gather.22
  316.9 76.7 all-gather.20
  428.1 13.2 reduce-scatter.13
  446.4 11.8 all-gather.24
  463.0 82.7 reduce-scatter.21
  548.6 176.9 reduce-scatter.23
  728.4 180.2 reduce-scatter.25
  910.8 14.4 reduce-scatter.17
  928.1 137.4 reduce-scatter.19
  1068.2 137.1 reduce-scatter.27
  1210.5 126.4 all-reduce.22
  1342.3 111.2 all-reduce.12
  1462.6 129.7 all-reduce.24
  1600.4 129.6 all-reduce.26
  1735.4 111.2 all-reduce.14
  1851.9 129.7 all-reduce.28
  1986.8 111.2 all-reduce.16
  2103.3 129.7 all-reduce.30
  2238.3 111.2 all-reduce.18
  2356.3 111.4 all-reduce.20
  (3 shorter events, 26.3 us)
where the time goes:
time: 2490 us; the launch traced here: 2480 us
  waiting for transfers between devices  1890 us (76%)
  matrix products  268 us (11%)
  blocking collectives  163 us (7%)
  other arithmetic  86.2 us (3%)
  local copies, waits for them, and re-layouts  45.6 us (2%)
    psum x5, waiting for transfers between devices, feed_gram(): return lax.psum(block_gram(ortho), ('dp', 'tensor'))  639 us
    psum x4, waiting for transfers between devices, per_device(): head_grams.append(lax.psum(block_gram(head_ortho), 'dp'))  436 us
    reduce_scatter x1, waiting for transfers between devices, per_device(): lax.psum_scatter(shrink_grad, 'dp', scatter_dimension=0, tiled=True)  177 us
    reduce_scatter x1, waiting for transfers between devices, per_device(): lax.psum_scatter(triple_grad, 'dp', scatter_dimension=0, tiled=True)  133 us
    unnamed x28, waiting for transfers between devices  128 us
    psum x1, waiting for transfers between devices, per_device(): lax.psum((block_gram(head_update), bias_grad_local), 'dp')  117 us
    all_gather x1, waiting for transfers between devices, per_device(): lax.all_gather(low_shrink, 'dp', axis=0, tiled=True)  80.1 us
    psum x1, blocking collectives, per_device(): lax.psum((block_gram(head_update), bias_grad_local), 'dp')  77.8 us
  transfers between devices with their start and end apart: 27, of which 25 were waited for; matrix products, arithmetic and copies ran while one was open for 13% of the time, Pallas kernels for 0%

commit v1 on v0

--- a/solution.py
+++ b/solution.py
@@ -132,14 +132,32 @@
     return jnp.einsum("rbi,rbj->bij", ortho, ortho, precision=highest)
 
 
-def block_step(ortho, gram):
-    product = jnp.einsum("rbi,bij->rbj", ortho, gram, precision=highest)
-    twice = jnp.einsum("rbi,bij->rbj", product, gram, precision=highest)
-    return first_coef * ortho + second_coef * product + third_coef * twice
-
-
-def feed_gram(ortho):
-    return lax.psum(block_gram(ortho), ("dp", "tensor"))
+def small_dot(left, right):
+    return jnp.einsum("bij,bjk->bik", left, right, precision=highest)
+
+
+def gram_factor(raw):
+    scale = jnp.sqrt(jnp.trace(raw, axis1=1, axis2=2)) + muon_eps
+    eye = jnp.eye(raw.shape[-1], dtype=jnp.float32)[None]
+    gram = raw / (scale * scale)[:, None, None]
+    factor = None
+    for turn in range(5):
+        step = first_coef * eye + second_coef * gram + third_coef * small_dot(gram, gram)
+        factor = step if factor is None else small_dot(factor, step)
+        if turn < 4:
+            gram = small_dot(step, small_dot(gram, step))
+    return factor / scale[:, None, None]
+
+
+def shared_factor(partial, axes):
+    count = partial.shape[0]
+    parts = lax.axis_size(axes)
+    extra = -count % parts
+    if extra:
+        partial = jnp.pad(partial, ((0, extra), (0, 0), (0, 0)))
+    raw = lax.psum_scatter(partial, axes, scatter_dimension=0, tiled=True)
+    factor = lax.all_gather(gram_factor(raw), axes, axis=0, tiled=True)
+    return factor[:count]
 
 
 def adam_step(param, gradient, first, second, count):
@@ -192,16 +210,40 @@
     low_expand = expand_weight.astype(jnp.bfloat16)
     low_shrink = shrink_weight.astype(jnp.bfloat16)
     low_shift = expand_bias.astype(jnp.bfloat16)
-    triple, dense, expand, shrink, expand_shift = (
+    low_small = small_params.astype(jnp.bfloat16)
+    other_small = lax.ppermute(
+        low_small, "tensor", [(i, (i + 1) % pieces) for i in range(pieces)]
+    )
+    pair_small = jnp.where(
+        here == 0,
+        jnp.concatenate((low_small, other_small), axis=1),
+        jnp.concatenate((other_small, low_small), axis=1),
+    )
+    extras = jnp.concatenate((low_shift, pair_small.reshape(-1)))
+    extra_rows = -(-extras.shape[0] // head_cols)
+    extras = jnp.pad(extras, (0, extra_rows * head_cols - extras.shape[0]))
+    dense_rows = low_dense.shape[0]
+    packed = lax.all_gather(
+        jnp.concatenate((low_dense, extras.reshape(extra_rows, head_cols)), axis=0), "dp", axis=0
+    )
+    groups = packed.shape[0]
+    dense = packed[:, :dense_rows].reshape(groups * dense_rows, head_cols)
+    packed_extras = packed[:, dense_rows:].reshape(groups, extra_rows * head_cols)
+    shifts = low_shift.shape[0]
+    expand_shift = packed_extras[:, :shifts].reshape(-1)
+    smalls = pair_small.size
+    small = (
+        packed_extras[:, shifts : shifts + smalls]
+        .reshape((groups,) + pair_small.shape)
+        .transpose(1, 0, 2)
+        .reshape(pair_small.shape[0], width)
+        .astype(jnp.float32)
+    )
+    triple, expand, shrink = (
         lax.all_gather(low_triple, "dp", axis=0, tiled=True),
-        lax.all_gather(low_dense, "dp", axis=0, tiled=True),
         lax.all_gather(low_expand, "dp", axis=0, tiled=True),
         lax.all_gather(low_shrink, "dp", axis=0, tiled=True),
-        lax.all_gather(low_shift, "dp", axis=0, tiled=True),
-    )
-    small = lax.all_gather(
-        small_params.astype(jnp.bfloat16), ("dp", "tensor"), axis=1, tiled=True
-    ).astype(jnp.float32)
+    )
     query_shift = lax.optimization_barrier(query_value_bias.astype(jnp.bfloat16)).astype(
         jnp.float32
     )
@@ -334,20 +376,11 @@
         .transpose(1, 0, 2, 3)
         .reshape(feed_rows, 2 * feed_blocks, HD)
     )
-    raw_head, bias_sum = lax.psum((block_gram(head_update), bias_grad_local), "dp")
-    head_scale = jnp.sqrt(jnp.trace(raw_head, axis1=1, axis2=2)) + muon_eps
-    head_ortho = head_update / head_scale[None, :, None]
-    head_grams = [raw_head / (head_scale * head_scale)[:, None, None]]
-    raw_feed = feed_gram(feed_update)
-    feed_scale = jnp.sqrt(jnp.trace(raw_feed, axis1=1, axis2=2)) + muon_eps
-    feed_ortho = feed_update / feed_scale[None, :, None]
-    feed_grams = [raw_feed / (feed_scale * feed_scale)[:, None, None]]
-    for turn in range(5):
-        if turn >= len(head_grams):
-            head_grams.append(lax.psum(block_gram(head_ortho), "dp"))
-            feed_grams.append(feed_gram(feed_ortho))
-        head_ortho = block_step(head_ortho, head_grams[turn])
-        feed_ortho = block_step(feed_ortho, feed_grams[turn])
+    bias_sum = lax.psum(bias_grad_local, "dp")
+    head_factor = shared_factor(block_gram(head_update), "dp")
+    feed_factor = shared_factor(block_gram(feed_update), ("dp", "tensor"))
+    head_ortho = jnp.einsum("rbi,bij->rbj", head_update, head_factor, precision=highest)
+    feed_ortho = jnp.einsum("rbi,bij->rbj", feed_update, feed_factor, precision=highest)
     head_change = head_ortho * (muon_rate * math.sqrt(max(1.0, width / HD)))
     triple_new = query_key_value - head_change[:, : 3 * heads_here].reshape(rows_here, 3, head_cols)
     dense_new = dense_weight - head_change[:, 3 * heads_here :].reshape(rows_here, head_cols)

time: 2490 us -> 1490 us (0.60)
  waiting for transfers between devices: 1890 us -> 945 us
  matrix products: 268 us -> 215 us
    psum x10 -> x0, waiting for transfers between devices: 1190 us -> none  [the longest x5 639 us: feed_gram(): return lax.psum(block_gram(ortho), ('dp', 'tensor'))]
    reduce_scatter x1, waiting for transfers between devices: 0.02 us -> 162 us  [per_device(): lax.psum_scatter(expand_grad, 'dp', scatter_dimension=0, tiled=True)]
    reduce_scatter x0 -> x2, waiting for transfers between devices: none -> 75.3 us  [shared_factor(): raw = lax.psum_scatter(partial, axes, scatter_dimension=0, tiled=True)]
    reduce_scatter x1, waiting for transfers between devices: 133 us -> 75.9 us  [per_device(): lax.psum_scatter(triple_grad, 'dp', scatter_dimension=0, tiled=True)]
    all_gather x1, waiting for transfers between devices: 13.9 us -> 57.1 us  [per_device(): lax.all_gather(jnp.concatenate((low_dense, extras.reshape(extra_rows, hea...]
    all_gather x1, waiting for transfers between devices: 30.1 us -> 70.8 us  [per_device(): lax.all_gather(low_expand, 'dp', axis=0, tiled=True)]
    dot_general x20 -> x36, matrix products: 43.3 us -> 13.3 us  [the longest x34 9.58 us: small_dot(): return jnp.einsum('bij,bjk->bik', left, right, precision=highest)]
    unnamed x28 -> x20, waiting for transfers between devices: 128 us -> 130 us
  transfers between devices with their start and end apart: 27 -> 20, of which waited for: 25 -> 14; matrix products, arithmetic and copies ran while one was open for 13% -> 17% of each run, Pallas kernels for 0% -> 0%
where the time goes in v1:
time: 1490 us
  waiting for transfers between devices  945 us (63%)
  matrix products  215 us (14%)
  blocking collectives  164 us (11%)
  other arithmetic  89.4 us (6%)
  local copies, waits for them, and re-layouts  46.3 us (3%)
  between operations  18.1 us (1%)
    reduce_scatter x1, waiting for transfers between devices, per_device(): lax.psum_scatter(shrink_grad, 'dp', scatter_dimension=0, tiled=True)  181 us
    reduce_scatter x1, waiting for transfers between devices, per_device(): lax.psum_scatter(expand_grad, 'dp', scatter_dimension=0, tiled=True)  162 us
    unnamed x20, waiting for transfers between devices  130 us
    all_gather x2, blocking collectives, shared_factor(): factor = lax.all_gather(gram_factor(raw), axes, axis=0, tiled=True)  86.3 us
    all_gather x1, waiting for transfers between devices, per_device(): lax.all_gather(low_shrink, 'dp', axis=0, tiled=True)  80.1 us
    psum x1, blocking collectives, per_device(): bias_sum = lax.psum(bias_grad_local, 'dp')  77.7 us
    reduce_scatter x1, waiting for transfers between devices, per_device(): lax.psum_scatter(triple_grad, 'dp', scatter_dimension=0, tiled=True)  75.9 us
    reduce_scatter x2, waiting for transfers between devices, shared_factor(): raw = lax.psum_scatter(partial, axes, scatter_dimension=0, tiled=True)  75.3 us
  transfers between devices with their start and end apart: 20, of which 14 were waited for; matrix products, arithmetic and copies ran while one was open for 17% of the time, Pallas kernels for 0%

profile of v1, /device:TPU:0, one launch (start us, length us, event | category | flops | bytes accessed | tf_op | source)
XLA Modules:
  0.0 1486.7 jit_solution(3133135273251427609)
XLA Ops:
  12.9 57.1 %all-gather.26.cloned.1.call-done = bf16[16,65,512]{2,1,0:T(8,128)(2,1)} async-done(((bf16[1,65,512]{2,1,0:T(8,128)(2,1)}), bf16[16,65,512]{2,1,0:T(8,128)(2,1)}) %all-gather.26.cloned.1.call-update) | async-done | bytes 1064976 | tf_op jit(solution)/shard_map/all_gather | solution.py:226
  83.4 72.4 %all-gather.14.cloned.1.call-done = bf16[1024,3,512]{2,0,1:T(8,128)(2,1)} async-done(((bf16[64,3,512]{2,0,1:T(8,128)(2,1)}), bf16[1024,3,512]{2,0,1:T(8,128)(2,1)}) %all-gather.14.cloned.1.call-update) | async-done | bytes 3145744 | tf_op jit(solution)/shard_map/all_gather | solution.py:243
  163.9 30.6 %while.28 = (s32[]{:T(128)}, bf16[2,512,8,64]{1,3,2,0:T(8,128)(2,1)}, f32[2,8,512]{2,1,0:T(8,128)S(1)}, s32[2]{0:T(128)S(1)}, s32[]{:T(128)}, /*index=5*/bf16[10...) while((s32[]{:T(128)}, ...), condition=%wide.region_5.6_spmd.clone, body=%wide.region_2.5_spmd.clone.sunk | while | flops 1118041600 | bytes 58860780 | solution.py:80
  222.4 70.8 %all-gather.18.cloned.1.call-done = bf16[2048,1024]{1,0:T(8,128)(2,1)} async-done(((bf16[128,1024]{1,0:T(8,128)(2,1)}), bf16[2048,1024]{1,0:T(8,128)(2,1)}) %all-gather.18.cloned.1.call-update) | async-done | bytes 4194320 | tf_op jit(solution)/shard_map/all_gather | solution.py:244
  293.2 11.2 all-gather.16.cloned.1.call-done
  304.3 13.8 multiply_convert_fusion.1
  318.2 80.1 %all-gather.20.cloned.1.call-done = bf16[2048,1024]{1,0:T(8,128)(2,1)} async-done(((bf16[128,1024]{1,0:T(8,128)(2,1)}), bf16[2048,1024]{1,0:T(8,128)(2,1)}) %all-gather.20.cloned.1.call-update) | async-done | bytes 4194320 | tf_op jit(solution)/shard_map/all_gather | solution.py:245
  398.4 13.4 convert_reduce_fusion
  420.0 9.9 fusion.96
  433.7 12.3 reduce-scatter.16.cloned.1.call-done
  451.0 11.0 fusion.99
  482.4 162.4 %reduce-scatter.26.cloned.1.call-done = f32[128,1024]{1,0:T(8,128)} async-done(((f32[2048,1024]{1,0:T(8,128)}), f32[128,1024]{1,0:T(8,128)}) %reduce-scatter.26.cloned.1.call-update) | async-done | bytes 524304 | tf_op jit(solution)/shard_map/reduce_scatter | solution.py:352
  646.9 181.0 %reduce-scatter.28.cloned.1.call-done = f32[128,1024]{1,0:T(8,128)} async-done(((f32[2048,1024]{1,0:T(8,128)}), f32[128,1024]{1,0:T(8,128)}) %reduce-scatter.28.cloned.1.call-update) | async-done | bytes 524304 | tf_op jit(solution)/shard_map/reduce_scatter | solution.py:353
  837.5 121.3 %while.29 = (s32[]{:T(128)}, f32[1024,8,64]{0,2,1:T(8,128)S(1)}, f32[1024,8,64]{0,2,1:T(8,128)}, bf16[2,512,8,64]{1,3,2,0:T(8,128)(2,1)}, s32[2]{0:T(128)S(1)}, ...) while((s32[]{:T(128)}, f32[1024,8,64]{0,2,1:T(8,128)S(1)}, ...), condition=%wide.region_15.16_spmd.clone, body=%wide.region_13.15_spmd.clone.sunk | while | flops 2735732224 | bytes 212427632 | solution.py:121
  851.5 13.9 multiply_reduce_fusion.7
  865.4 15.0 %multiply_convert_fusion.4 = bf16[8,512,1024]{2,1,0:T(8,128)(2,1)} fusion(f32[8,512,1024]{2,1,0:T(8,128)} %get-tuple-element.520, f32[8,512,1024]{2,1,0:T(8,128)} %fusion.253, f32[8,512]{1,0:T(8,128)S(1)} %get-tuple-element.521), kind=kLoop, calls=%fused_computation.19.clone.1 | loop fusion | flops 12582912 | bytes 41959424 | tf_op jit(solution)/shard_map/while/body/eval_jaxpr/convert_element_type | solution.py:100
  911.8 14.0 multiply_reduce_fusion.7
  925.8 14.9 %multiply_convert_fusion.4 = bf16[8,512,1024]{2,1,0:T(8,128)(2,1)} fusion(f32[8,512,1024]{2,1,0:T(8,128)} %get-tuple-element.520, f32[8,512,1024]{2,1,0:T(8,128)} %fusion.253, f32[8,512]{1,0:T(8,128)S(1)} %get-tuple-element.521), kind=kLoop, calls=%fused_computation.19.clone.1 | loop fusion | flops 12582912 | bytes 41959424 | tf_op jit(solution)/shard_map/while/body/eval_jaxpr/convert_element_type | solution.py:100
  995.5 77.7 %all-reduce.1 = (f32[2,512]{1,0:T(2,128)S(1)}, f32[2048]{0:T(1024)S(1)}) all-reduce(f32[2,512]{1,0:T(2,128)S(1)} %convert_reduce_fusion.1, f32[2048]{0:T(1024)S(1)} %copy-done.48), channel_id=1, replica_groups=mesh['dp'=16,'tensor'=2] {'dp'}, use_global_device_ids=true, to_apply=%region_24.25 | all-reduce | flops 3072 | bytes 24576 | tf_op jit(solution)/shard_map/psum | solution.py:379
  1082.8 43.9 %all-gather.1 = f32[2048,64]{1,0:T(8,128)S(1)} all-gather(f32[64,64]{1,0:T(8,128)S(1)} %convolution_divide_fusion.1), channel_id=3, replica_groups=mesh['dp'=16,'tensor'=2] {'dp','tensor'}, dimensions={0}, use_global_device_ids=true | all-gather | bytes 540672 | tf_op jit(solution)/shard_map/all_gather | solution.py:159
  1134.7 75.9 %reduce-scatter.22.cloned.1.call-done = f32[64,3,512]{2,0,1:T(8,128)} async-done(((f32[1024,3,512]{2,0,1:T(8,128)}), f32[64,3,512]{2,0,1:T(8,128)}) %reduce-scatter.22.cloned.1.call-update) | async-done | bytes 393232 | tf_op jit(solution)/shard_map/reduce_scatter | solution.py:350
  1220.3 129.8 %reduce-scatter.34.cloned.1.call-done = f32[32,6]{1,0:T(8,128)} async-done(((f32[1024,6]{1,0:T(8,128)}), f32[32,6]{1,0:T(8,128)}) %reduce-scatter.34.cloned.1.call-update) | async-done | bytes 784
  1351.6 75.3 %reduce-scatter.30.cloned.1.call-done = f32[2,64,64]{2,1,0:T(8,128)} async-done(((f32[32,64,64]{2,1,0:T(8,128)}), f32[2,64,64]{2,1,0:T(8,128)}) %reduce-scatter.30.cloned.1.call-update) | async-done | bytes 32784 | tf_op jit(solution)/shard_map/reduce_scatter | solution.py:158
  1433.1 42.4 %all_gather.42 = f32[32,64,64]{2,1,0:T(8,128)S(1)} all-gather(f32[2,64,64]{2,1,0:T(8,128)S(1)} %convolution_divide_fusion), channel_id=1, replica_groups=mesh['dp'=16,'tensor'=2] {'dp'}, dimensions={0}, use_global_device_ids=true | all-gather | bytes 557056 | tf_op jit(solution)/shard_map/all_gather | solution.py:159
  (366 shorter events, 263.6 us)
Async XLA Ops:
  7.2 62.9 %all-gather.26.cloned.1.call-start = ((), (), s32[]{:S(2)}) async-start(), calls=%async_computation.28 | async-start | bytes 1253376 | tf_op jit(solution)/shard_map/all_gather | solution.py:226
  8.0 2.1 collective-permute-start
  11.0 72.5 %all-gather.12.cloned.1.call-start = ((), (), s32[]{:S(2)}) async-start(), calls=%async_computation.11 | async-start | bytes 3145728 | tf_op jit(solution)/shard_map/all_gather | solution.py:253
  74.0 81.8 %all-gather.14.cloned.1.call-start = ((), (), s32[]{:S(2)}) async-start(), calls=%async_computation.12 | async-start | bytes 3342336 | tf_op jit(solution)/shard_map/all_gather | solution.py:243
  74.8 138.3 %reduce-scatter.14.cloned.1.call-start = ((), (), s32[]{:S(2)}) async-start(), calls=%async_computation.13 | async-start | bytes 6291456 | tf_op jit(solution)/shard_map/reduce_scatter | solution.py:267
  202.2 90.9 %all-gather.18.cloned.1.call-start = ((), (), s32[]{:S(2)}) async-start(), calls=%async_computation.15 | async-start | bytes 4456448 | tf_op jit(solution)/shard_map/all_gather | solution.py:244
  204.0 100.3 %all-gather.16.cloned.1.call-start = ((), (), s32[]{:S(2)}) async-start(), calls=%async_computation.14 | async-start | bytes 3145728 | tf_op jit(solution)/shard_map/all_gather | solution.py:279
  216.8 101.4 %all-gather.22.cloned.1.call-start = ((), (), s32[]{:S(2)}) async-start(), calls=%async_computation.18 | async-start | bytes 3145728 | tf_op jit(solution)/shard_map/all_gather | solution.py:291
  219.4 179.0 %all-gather.20.cloned.1.call-start = ((), (), s32[]{:S(2)}) async-start(), calls=%async_computation.16 | async-start | bytes 4456448 | tf_op jit(solution)/shard_map/all_gather | solution.py:245
  221.3 209.4 %reduce-scatter.18.cloned.1.call-start = ((), (), s32[]{:S(2)}) async-start(), calls=%async_computation.19 | async-start | bytes 6291456 | tf_op jit(solution)/shard_map/reduce_scatter | solution.py:302
  419.7 26.3 %reduce-scatter.16.cloned.1.call-start = ((), (), s32[]{:S(2)}) async-start(), calls=%async_computation.17 | async-start | bytes 6291456 | tf_op jit(solution)/shard_map/reduce_scatter | solution.py:285
  429.9 42.7 %all-gather.24.cloned.1.call-start = ((), (), s32[]{:S(2)}) async-start(), calls=%async_computation.20 | async-start | bytes 3145728 | tf_op jit(solution)/shard_map/all_gather | solution.py:312
  450.9 193.8 %reduce-scatter.26.cloned.1.call-start = ((), (), s32[]{:S(2)}) async-start(), calls=%async_computation.24 | async-start | bytes 8912896 | tf_op jit(solution)/shard_map/reduce_scatter | solution.py:352
  462.0 365.9 %reduce-scatter.28.cloned.1.call-start = ((), (), s32[]{:S(2)}) async-start(), calls=%async_computation.25 | async-start | bytes 8912896 | tf_op jit(solution)/shard_map/reduce_scatter | solution.py:353
  472.6 601.9 %reduce-scatter.24.cloned.1.call-start = ((), (), s32[]{:S(2)}) async-start(), calls=%async_computation.23 | async-start | bytes 2228224 | tf_op jit(solution)/shard_map/reduce_scatter | solution.py:351
  478.1 598.1 %reduce-scatter.32.cloned.1.call-start = ((), (), s32[]{:S(2)}) async-start(), calls=%async_computation.27 | async-start | bytes 1081344 | tf_op jit(solution)/shard_map/reduce_scatter | solution.py:158
  478.1 166.6 %copy-start.24 = (f32[128,1024]{1,0:T(8,128)S(1)}, f32[128,1024]{1,0:T(8,128)}, u32[]{:S(2)}) copy-start(f32[128,1024]{1,0:T(8,128)} %param.37) | copy-start | bytes 1572868
  835.9 294.9 %reduce-scatter.20.cloned.1.call-start = ((), (), s32[]{:S(2)}) async-start(), calls=%async_computation.21 | async-start | bytes 6291456 | tf_op jit(solution)/shard_map/reduce_scatter | solution.py:331
  979.9 230.6 %reduce-scatter.22.cloned.1.call-start = ((), (), s32[]{:S(2)}) async-start(), calls=%async_computation.22 | async-start | bytes 6684672 | tf_op jit(solution)/shard_map/reduce_scatter | solution.py:350
  988.3 361.8 %reduce-scatter.34.cloned.1.call-start = ((), (), s32[]{:S(2)}) async-start(), calls=%async_computation.29 | async-start | bytes 540672
  1134.6 292.2 %reduce-scatter.30.cloned.1.call-start = ((), (), s32[]{:S(2)}) async-start(), calls=%async_computation.26 | async-start | bytes 1114112 | tf_op jit(solution)/shard_map/reduce_scatter | solution.py:158
  1216.0 134.9 %copy-start.47 = (f32[6,32]{1,0:T(8,128)S(1)}, f32[6,32]{1,0:T(8,128)}, u32[]{:S(2)}) copy-start(f32[6,32]{1,0:T(8,128)} %param.34) | copy-start | bytes 2308
  1216.1 134.9 %copy-start.51 = (f32[6,32]{1,0:T(8,128)S(1)}, f32[6,32]{1,0:T(8,128)}, u32[]{:S(2)}) copy-start(f32[6,32]{1,0:T(8,128)} %param.39) | copy-start | bytes 2308
  1216.1 134.9 %copy-start.52 = (f32[6,32]{1,0:T(8,128)S(1)}, f32[6,32]{1,0:T(8,128)}, u32[]{:S(2)}) copy-start(f32[6,32]{1,0:T(8,128)} %param.40) | copy-start | bytes 2308
  (58 other events, 1282.3 us)
Sparse Core Ops, SparseCore 0:
  11.4 58.6 all-gather.25
  74.1 9.2 all-gather.11
  86.8 69.0 all-gather.13
  202.4 10.6 reduce-scatter.13
  216.3 76.8 all-gather.17
  295.1 9.1 all-gather.15
  306.5 11.7 all-gather.21
  321.6 76.7 all-gather.19
  419.9 10.6 reduce-scatter.17
  432.7 13.2 reduce-scatter.15
  451.1 11.8 all-gather.23
  465.7 179.0 reduce-scatter.25
  647.6 180.2 reduce-scatter.27
  830.6 84.0 reduce-scatter.23
  916.8 133.2 reduce-scatter.31
  1052.2 7.9 reduce-scatter.19
  1062.9 147.5 reduce-scatter.21
  1212.6 137.4 reduce-scatter.33
  1352.4 74.4 reduce-scatter.29
